TPU v7x, 128 devices: a whole 4x4x4 slice. The times are simulated.
128 devices in a mesh: tok: 8 (over x, z_hi), feat: 16 (over y, z_lo, core).
Axes of the slice: x: 4, y: 4, z: 4 (z_hi: 2, z_lo: 2; z = z_hi * 2 + z_lo), core: 2. Of those that a mesh axis runs over, the one named last changes fastest.
Arguments:
- resid: bfloat16 [2048, 8192], P(None, ('tok', 'feat')), may hold values from -6 to 6
- resid_grad: bfloat16 [2048, 8192], P(None, ('tok', 'feat')), may hold values from -6 to 6
- active: int32 [16, 20], P('tok'), may hold values from 0 to 79, all different within a row
- w_enc: bfloat16 [8192, 10240], P(None, 'feat'), may hold values from -0.0625 to 0.0625
- b_enc: float32 [10240], P('feat'), may hold values from -3 to 3
- w_dec: bfloat16 [10240, 8192], P('feat'), may hold values from -0.25 to 0.25
- b_dec: float32 [8192], P('feat'), may hold values from -3 to 3
Outputs:
- feature_attr: float32 [2048, 10240], P('tok', 'feat')
- error: float32 [2048, 8192], P('tok', 'feat')
- error_attr: float32 [2048], P('tok')
Inputs may be any that keep to these rules, and one draw needn't show every extreme that they name: `active`: each row lists 20 different feature blocks; every block is listed by some tile.
All inputs are finite; a program needn't handle non-finite values.
Results may differ from a plain program's by a relative error of at most 0.012.
Values may be sent and summed in bfloat16 or wider, within the bound.
A program may use at most 128 MiB of HBM per device.

v0:
```python
import jax
import jax.numpy as jnp
from jax import lax
from jax.sharding import PartitionSpec as P

BLOCK = 128
TILE = 128


def per_device(resid, resid_grad, active, w_enc, b_enc, w_dec, b_dec):
    n_feat = lax.axis_size("feat")
    width = resid.shape[1]
    cols_x, cols_g = (
        lax.all_gather(resid[:, None, :], "feat", axis=1, tiled=True),
        lax.all_gather(resid_grad[:, None, :], "feat", axis=1, tiled=True),
    )
    total = cols_x.shape[0]
    cols_x = cols_x.reshape(total, n_feat * width)
    cols_g = cols_g.reshape(total, n_feat * width)
    rows_x, rows_g = (
        lax.all_to_all(cols_x, "tok", split_axis=0, concat_axis=1, tiled=True),
        lax.all_to_all(cols_g, "tok", split_axis=0, concat_axis=1, tiled=True),
    )
    tok_rows = rows_x.shape[0]
    feat_dev = w_enc.shape[1]
    blocks = feat_dev // BLOCK
    tiles_dev = active.shape[0]
    block_ids = lax.axis_index("feat") * blocks + jnp.arange(blocks, dtype=jnp.int32)
    hits = jnp.any(active[:, :, None] == block_ids[None, None, :], axis=1).astype(jnp.float32)
    pre = jnp.dot(rows_x, w_enc, preferred_element_type=jnp.float32) + b_enc
    shaped = jnp.maximum(pre, 0.0).reshape(tiles_dev, TILE, blocks, BLOCK) * hits[:, None, :, None]
    acts = shaped.reshape(tok_rows, feat_dev).astype(jnp.bfloat16)
    partial_recon = jnp.dot(acts, w_dec, preferred_element_type=jnp.float32)
    recon_share = lax.psum_scatter(
        partial_recon.astype(jnp.bfloat16), "feat", scatter_dimension=1, tiled=True
    ).astype(jnp.float32)
    share = recon_share.shape[1]
    start = lax.axis_index("feat") * share
    own_x = lax.dynamic_slice_in_dim(rows_x, start, share, 1)
    own_g = lax.dynamic_slice_in_dim(rows_g, start, share, 1)
    recon = recon_share + b_dec
    error = own_x.astype(jnp.float32) - recon
    local_terms = jnp.sum(error * own_g.astype(jnp.float32), axis=1)
    error_attr = lax.psum(local_terms, "feat")
    proj = lax.dot_general(
        rows_g, w_dec, (((1,), (1,)), ((), ())), preferred_element_type=jnp.float32
    )
    feature_attr = acts.astype(jnp.float32) * proj
    return (feature_attr, error, error_attr)


def solution(mesh):
    placed = (
        P(None, ("tok", "feat")),
        P(None, ("tok", "feat")),
        P("tok", None),
        P(None, "feat"),
        P("feat"),
        P("feat", None),
        P("feat"),
    )
    return jax.shard_map(
        per_device,
        mesh=mesh,
        in_specs=placed,
        out_specs=(P("tok", "feat"), P("tok", "feat"), P("tok")),
        check_vma=False,
    )
```

profile of v0, /device:TPU:0, one launch (start us, length us, event | category | flops | bytes accessed | tf_op | source)
XLA Modules:
  0.0 284.6 jit_solution(3607693962824944712)
XLA Ops:
  7.2 0.7 all-gather.5.cloned.1.call-update
  7.9 0.0 all-gather.7.cloned.1.call-start
  7.9 0.7 all-gather.7.cloned.1.call-update
  8.6 40.8 %all-gather.5.cloned.1.call-done = bf16[2048,1024]{0,1:T(8,128)(2,1)} async-done(((bf16[2048,64]{0,1:T(8,128)(2,1)}), bf16[2048,1024]{0,1:T(8,128)(2,1)}) %all-gather.5.cloned.1.call-update) | async-done | bytes 4194320 | tf_op jit(solution)/shard_map/all_gather | solution.py:14
  49.5 6.4 %copy.20 = bf16[2048,1024]{1,0:T(8,128)(2,1)} copy(bf16[2048,1024]{0,1:T(8,128)(2,1)} %all-gather.5.cloned.1.call-done) | data formatting | bytes 8388608 | tf_op jit(solution)/shard_map/all_gather | solution.py:14
  55.8 6.6 %all-to-all-start = ((bf16[8,256,1024]{2,1,0:T(8,128)(2,1)}), bf16[8,256,1024]{2,1,0:T(8,128)(2,1)}, u32[]{:S(2)}, u32[]{:S(2)}) async-start(bf16[8,256,1024]{2,1,0:T(8,128)(2,1)} %bitcast.21), calls=%async_computation | async-start | bytes 8388608 | tf_op jit(solution)/shard_map/all_to_all | solution.py:21
  62.5 0.2 compare_reduce_fusion
  62.7 0.1 copy.22
  62.8 0.2 mul.24
  63.1 0.2 copy.23
  63.4 59.7 %all-to-all-done = bf16[8,256,1024]{2,1,0:T(8,128)(2,1)} async-done(((bf16[8,256,1024]{2,1,0:T(8,128)(2,1)}), bf16[8,256,1024]{2,1,0:T(8,128)(2,1)}, u32[]{:S(2)}, u32[]{:S(2)}) %all-to-all-start) | async-done | bytes 4194336 | tf_op jit(solution)/shard_map/all_to_all | solution.py:21
  123.1 2.9 %copy.26 = bf16[8,32,8,1024]{3,2,0,1:T(8,128)(2,1)S(1)} copy(bf16[8,32,8,1024]{3,2,1,0:T(8,128)(2,1)} %bitcast.4) | data formatting | bytes 8388608 | tf_op jit(solution)/shard_map/all_to_all | solution.py:21
  126.0 2.0 copy-done
  127.9 6.5 %fusion.2 = bf16[256,640]{1,0:T(8,128)(2,1)S(1)} fusion(f32[256,640]{1,0:T(8,128)S(1)} %copy.23, bf16[256,8192]{1,0:T(8,128)(2,1)S(1)} %bitcast.23, bf16[8192,640]{1,0:T(8,128)(2,1)} %param.10, f32[640]{0:T(1024)S(1)} %copy-done.4), kind=kOutput, calls=%fused_computation.5 | convolution fusion | flops 2685009920 | bytes 15665664 | tf_op jit(solution)/shard_map/dot_general | solution.py:30
  134.4 4.9 %convolution_convert_fusion = bf16[256,8192]{1,0:T(8,128)(2,1)} fusion(bf16[256,640]{1,0:T(8,128)(2,1)S(1)} %fusion.2, bf16[640,8192]{1,0:T(8,128)(2,1)S(1)} %bitcast.30), kind=kOutput, calls=%fused_computation | convolution fusion | flops 2686451712 | bytes 15007744 | tf_op jit(solution)/shard_map/dot_general | solution.py:33
  139.4 6.4 %copy.24 = bf16[2048,1024]{1,0:T(8,128)(2,1)} copy(bf16[2048,1024]{0,1:T(8,128)(2,1)} %all-gather.7.cloned.1.call-done) | data formatting | bytes 8388608 | tf_op jit(solution)/shard_map/all_gather | solution.py:15
  145.8 4.8 %all-to-all-start.1 = ((bf16[8,256,1024]{2,1,0:T(8,128)(2,1)}), bf16[8,256,1024]{2,1,0:T(8,128)(2,1)}, u32[]{:S(2)}, u32[]{:S(2)}) async-start(bf16[8,256,1024]{2,1,0:T(8,128)(2,1)} %bitcast.22), calls=%async_computation.1 | async-start | bytes 8388608 | tf_op jit(solution)/shard_map/all_to_all | solution.py:22
  150.6 61.9 %all-to-all-done.1 = bf16[8,256,1024]{2,1,0:T(8,128)(2,1)} async-done(((bf16[8,256,1024]{2,1,0:T(8,128)(2,1)}), bf16[8,256,1024]{2,1,0:T(8,128)(2,1)}, u32[]{:S(2)}, u32[]{:S(2)}) %all-to-all-start.1) | async-done | bytes 4194336 | tf_op jit(solution)/shard_map/all_to_all | solution.py:22
  212.5 2.7 copy.27
  215.2 1.9 copy-done.1
  217.1 7.1 %convolution_multiply_fusion = f32[256,640]{1,0:T(8,128)} fusion(bf16[256,8192]{1,0:T(8,128)(2,1)S(1)} %bitcast.25, bf16[640,8192]{1,0:T(8,128)(2,1)} %param.12, bf16[256,640]{1,0:T(8,128)(2,1)S(1)} %fusion.2), kind=kOutput, calls=%fused_computation.1 | convolution fusion | flops 2684682240 | bytes 15663104 | tf_op jit(solution)/shard_map/dot_general | solution.py:45
  224.2 22.1 %reduce-scatter.2.cloned.1.call-done = bf16[256,512]{1,0:T(8,128)(2,1)} async-done(((bf16[256,8192]{1,0:T(8,128)(2,1)}), bf16[256,512]{1,0:T(8,128)(2,1)}) %reduce-scatter.2.cloned.1.call-update) | async-done | bytes 262160 | tf_op jit(solution)/shard_map/reduce_scatter | solution.py:34
  246.3 2.0 multiply_reduce_fusion
  248.3 29.7 %psum.7 = f32[256]{0:T(256)} all-reduce(f32[256]{0:T(256)S(1)} %get-tuple-element.3), channel_id=1, replica_groups=mesh['tok'=8,'feat'=16] {'feat'}, use_global_device_ids=true, to_apply=%region_3.0 | all-reduce | flops 256 | bytes 2048 | tf_op jit(solution)/shard_map/psum | solution.py:44
  (22 shorter events, 0.2 us)
Async XLA Ops:
  7.2 42.3 %all-gather.5.cloned.1.call-start = ((), (), s32[]{:S(2)}) async-start(), calls=%async_computation.4 | async-start | bytes 4456448 | tf_op jit(solution)/shard_map/all_gather | solution.py:14
  7.9 131.5 %all-gather.7.cloned.1.call-start = ((), (), s32[]{:S(2)}) async-start(), calls=%async_computation.5 | async-start | bytes 4456448 | tf_op jit(solution)/shard_map/all_gather | solution.py:15
  55.8 6.7 %copy-start.3 = (s32[2,20]{1,0:T(2,128)S(1)}, s32[2,20]{1,0:T(2,128)}, u32[]{:S(2)}) copy-start(s32[2,20]{1,0:T(2,128)} %param.9) | copy-start | bytes 484
  55.8 67.2 %all-to-all-start = ((bf16[8,256,1024]{2,1,0:T(8,128)(2,1)}), bf16[8,256,1024]{2,1,0:T(8,128)(2,1)}, u32[]{:S(2)}, u32[]{:S(2)}) async-start(bf16[8,256,1024]{2,1,0:T(8,128)(2,1)} %bitcast.21), calls=%async_computation | async-start | bytes 8388608 | tf_op jit(solution)/shard_map/all_to_all | solution.py:21
  62.5 183.8 %reduce-scatter.2.cloned.1.call-start = ((), (), s32[]{:S(2)}) async-start(), calls=%async_computation.3 | async-start | bytes 4456448 | tf_op jit(solution)/shard_map/reduce_scatter | solution.py:34
  123.1 4.9 %copy-start.4 = (f32[640]{0:T(1024)S(1)}, f32[640]{0:T(1024)}, u32[]{:S(2)}) copy-start(f32[640]{0:T(1024)} %param.11) | copy-start | bytes 7684
  123.1 11.3 %slice-start = ((s8[10485760]{0:T(1024)(128)(4,1)}), s8[4194304]{0:T(1024)(128)(4,1)S(1)}, s32[]{:S(2)}) async-start(s8[10485760]{0:T(1024)(128)(4,1)} %bitcast.29), calls=%async_computation.6 | async-start | bytes 8388608
  126.0 2.0 copy-start
  127.9 6.5 %slice-start.1 = ((s8[10485760]{0:T(1024)(128)(4,1)}), s8[4194304]{0:T(1024)(128)(4,1)S(1)}, s32[]{:S(2)}) async-start(s8[10485760]{0:T(1024)(128)(4,1)} %bitcast.29), calls=%async_computation.7 | async-start | bytes 8388608
  127.9 6.5 %slice-start.2 = ((s8[10485760]{0:T(1024)(128)(4,1)}), s8[2097152]{0:T(1024)(128)(4,1)S(1)}, s32[]{:S(2)}) async-start(s8[10485760]{0:T(1024)(128)(4,1)} %bitcast.29), calls=%async_computation.8 | async-start | bytes 4194304
  145.8 66.7 %all-to-all-start.1 = ((bf16[8,256,1024]{2,1,0:T(8,128)(2,1)}), bf16[8,256,1024]{2,1,0:T(8,128)(2,1)}, u32[]{:S(2)}, u32[]{:S(2)}) async-start(bf16[8,256,1024]{2,1,0:T(8,128)(2,1)} %bitcast.22), calls=%async_computation.1 | async-start | bytes 8388608 | tf_op jit(solution)/shard_map/all_to_all | solution.py:22
  215.2 1.9 copy-start.1
  217.1 29.2 %copy-start.2 = (f32[512]{0:T(512)S(1)}, f32[512]{0:T(512)}, u32[]{:S(2)}) copy-start(f32[512]{0:T(512)} %param.13) | copy-start | bytes 6148
Sparse Core Ops, SparseCore 0:
  9.7 39.7 all-gather.4
  51.2 79.7 all-gather.6
  139.5 106.7 reduce-scatter.1
where the time goes:
time: 285 us
  waiting for transfers between devices  186 us (65%)
  blocking collectives  29.7 us (10%)
  local copies, waits for them, and re-layouts  22.8 us (8%)
  matrix products  18.5 us (6%)
  between operations  13.9 us (5%)
  starting transfers between devices  11.6 us (4%)
    all_to_all x1, waiting for transfers between devices, per_device(): lax.all_to_all(cols_g, 'tok', split_axis=0, concat_axis=1, tiled=True)  61.9 us
    all_to_all x1, waiting for transfers between devices, per_device(): lax.all_to_all(cols_x, 'tok', split_axis=0, concat_axis=1, tiled=True)  59.7 us
    all_gather x1, waiting for transfers between devices, per_device(): lax.all_gather(resid[:, None, :], 'feat', axis=1, tiled=True)  40.8 us
    psum x1, blocking collectives, per_device(): error_attr = lax.psum(local_terms, 'feat')  29.7 us
    reduce_scatter x1, waiting for transfers between devices, per_device(): lax.psum_scatter(partial_recon.astype(jnp.bfloat16), 'feat', scatter_dime...  22.1 us
    dot_general x1, matrix products, per_device(): lax.dot_general(rows_g, w_dec, (((1,), (1,)), ((), ())), preferred_elemen...  7.11 us
    all_to_all x1, starting transfers between devices, per_device(): lax.all_to_all(cols_x, 'tok', split_axis=0, concat_axis=1, tiled=True)  6.65 us
    dot_general x1, matrix products, per_device(): pre = jnp.dot(rows_x, w_enc, preferred_element_type=jnp.float32) + b_enc  6.46 us
  transfers between devices with their start and end apart: 5, of which 4 were waited for; matrix products, arithmetic and copies ran while one was open for 13% of the time, Pallas kernels for 0%

commit v1 on v0

--- a/solution.py
+++ b/solution.py
@@ -7,12 +7,18 @@
 TILE = 128
 
 
+def cycles_shape(inp, where_dim):
+    return jnp.concatenate(
+        lax.all_to_all(jnp.stack(lax.axis_size("feat") * [inp]), "feat", 0, 0), axis=where_dim
+    )
+
+
 def per_device(resid, resid_grad, active, w_enc, b_enc, w_dec, b_dec):
     n_feat = lax.axis_size("feat")
     width = resid.shape[1]
     cols_x, cols_g = (
         lax.all_gather(resid[:, None, :], "feat", axis=1, tiled=True),
-        lax.all_gather(resid_grad[:, None, :], "feat", axis=1, tiled=True),
+        cycles_shape(resid_grad[:, None, :], 1),
     )
     total = cols_x.shape[0]
     cols_x = cols_x.reshape(total, n_feat * width)

time: 285 us -> 321 us (1.13)
  waiting for transfers between devices: 186 us -> 214 us
  starting transfers between devices: 11.6 us -> 16.3 us
    all_to_all x0 -> x1, waiting for transfers between devices: none -> 38.3 us  [cycles_shape(): lax.all_to_all(jnp.stack(lax.axis_size('feat') * [inp]), 'feat', 0, 0)]
    reduce_scatter x1, waiting for transfers between devices: 22.1 us -> 8.23 us  [per_device(): lax.psum_scatter(partial_recon.astype(jnp.bfloat16), 'feat', scatter_dime...]
    all_gather x1 -> x0, local copies, waits for them, and re-layouts: 6.36 us -> none  [per_device(): lax.all_gather(resid_grad[:, None, :], 'feat', axis=1, tiled=True)]
    all_to_all x0 -> x1, starting transfers between devices: none -> 4.57 us  [cycles_shape(): lax.all_to_all(jnp.stack(lax.axis_size('feat') * [inp]), 'feat', 0, 0)]
    all_to_all x1, waiting for transfers between devices: 61.9 us -> 66.1 us  [per_device(): lax.all_to_all(cols_g, 'tok', split_axis=0, concat_axis=1, tiled=True)]
  transfers between devices with their start and end apart: 5 -> 5, of which waited for: 4 -> 5; matrix products, arithmetic and copies ran while one was open for 13% -> 10% of each run, Pallas kernels for 0% -> 0%
where the time goes in v1:
time: 321 us
  waiting for transfers between devices  214 us (67%)
  blocking collectives  31.1 us (10%)
  local copies, waits for them, and re-layouts  21.8 us (7%)
  matrix products  21.2 us (7%)
  starting transfers between devices  16.3 us (5%)
  between operations  14.2 us (4%)
    all_to_all x1, waiting for transfers between devices, per_device(): lax.all_to_all(cols_g, 'tok', split_axis=0, concat_axis=1, tiled=True)  66.1 us
    all_to_all x1, waiting for transfers between devices, per_device(): lax.all_to_all(cols_x, 'tok', split_axis=0, concat_axis=1, tiled=True)  59.2 us
    all_gather x1, waiting for transfers between devices, per_device(): lax.all_gather(resid[:, None, :], 'feat', axis=1, tiled=True)  41.6 us
    all_to_all x1, waiting for transfers between devices, cycles_shape(): lax.all_to_all(jnp.stack(lax.axis_size('feat') * [inp]), 'feat', 0, 0)  38.3 us
    psum x1, blocking collectives, per_device(): error_attr = lax.psum(local_terms, 'feat')  31.1 us
    dot_general x1, matrix products, per_device(): lax.dot_general(rows_g, w_dec, (((1,), (1,)), ((), ())), preferred_elemen...  9.72 us
    reduce_scatter x1, waiting for transfers between devices, per_device(): lax.psum_scatter(partial_recon.astype(jnp.bfloat16), 'feat', scatter_dime...  8.23 us
    all_to_all x1, starting transfers between devices, per_device(): lax.all_to_all(cols_x, 'tok', split_axis=0, concat_axis=1, tiled=True)  6.65 us
  transfers between devices with their start and end apart: 5, of which 5 were waited for; matrix products, arithmetic and copies ran while one was open for 10% of the time, Pallas kernels for 0%

profile of v1, /device:TPU:0, one launch (start us, length us, event | category | flops | bytes accessed | tf_op | source)
XLA Modules:
  0.0 320.9 jit_solution(16798643893637895423)
XLA Ops:
  7.2 0.7 all-gather.3.cloned.1.call-update
  7.9 41.6 %all-gather.3.cloned.1.call-done = bf16[2048,1024]{0,1:T(8,128)(2,1)} async-done(((bf16[2048,64]{0,1:T(8,128)(2,1)}), bf16[2048,1024]{0,1:T(8,128)(2,1)}) %all-gather.3.cloned.1.call-update) | async-done | bytes 4194320 | tf_op jit(solution)/shard_map/all_gather | solution.py:20
  49.5 6.4 %copy.20 = bf16[2048,1024]{1,0:T(8,128)(2,1)} copy(bf16[2048,1024]{0,1:T(8,128)(2,1)} %all-gather.3.cloned.1.call-done) | data formatting | bytes 8388608 | tf_op jit(solution)/shard_map/all_gather | solution.py:20
  55.9 6.6 %all-to-all-start = ((bf16[8,256,1024]{2,1,0:T(8,128)(2,1)}), bf16[8,256,1024]{2,1,0:T(8,128)(2,1)}, u32[]{:S(2)}, u32[]{:S(2)}) async-start(bf16[8,256,1024]{2,1,0:T(8,128)(2,1)} %bitcast.27), calls=%async_computation | async-start | bytes 8388608 | tf_op jit(solution)/shard_map/all_to_all | solution.py:27
  62.5 0.2 compare_reduce_fusion
  62.8 0.2 mul.24
  63.1 0.2 copy.23
  63.4 59.2 %all-to-all-done = bf16[8,256,1024]{2,1,0:T(8,128)(2,1)} async-done(((bf16[8,256,1024]{2,1,0:T(8,128)(2,1)}), bf16[8,256,1024]{2,1,0:T(8,128)(2,1)}, u32[]{:S(2)}, u32[]{:S(2)}) %all-to-all-start) | async-done | bytes 4194336 | tf_op jit(solution)/shard_map/all_to_all | solution.py:27
  122.5 2.4 stack.3
  125.0 4.6 %all-to-all-start.1 = ((bf16[16,2048,1,64]{1,3,2,0:T(8,128)(2,1)}), bf16[16,2048,1,64]{1,3,2,0:T(8,128)(2,1)}, u32[]{:S(2)}, u32[]{:S(2)}) async-start(bf16[16,2048,1,64]{1,3,2,0:T(8,128)(2,1)} %stack.3), calls=%async_computation.1 | async-start | bytes 8388608 | tf_op jit(solution)/shard_map/all_to_all | solution.py:12
  129.6 2.8 copy.28
  132.5 1.9 copy-done
  134.4 6.4 %fusion.2 = bf16[256,640]{1,0:T(8,128)(2,1)S(1)} fusion(f32[256,640]{1,0:T(8,128)S(1)} %copy.23, bf16[256,8192]{1,0:T(8,128)(2,1)S(1)} %bitcast.29, bf16[8192,640]{1,0:T(8,128)(2,1)} %param.10, f32[640]{0:T(1024)S(1)} %copy-done.4), kind=kOutput, calls=%fused_computation.5 | convolution fusion | flops 2685009920 | bytes 15665664 | tf_op jit(solution)/shard_map/dot_general | solution.py:36
  140.9 5.1 %convolution_convert_fusion = bf16[256,8192]{1,0:T(8,128)(2,1)} fusion(bf16[256,640]{1,0:T(8,128)(2,1)S(1)} %fusion.2, bf16[640,8192]{1,0:T(8,128)(2,1)S(1)} %bitcast.34), kind=kOutput, calls=%fused_computation | convolution fusion | flops 2686451712 | bytes 15007744 | tf_op jit(solution)/shard_map/dot_general | solution.py:39
  146.0 38.3 %all-to-all-done.1 = bf16[16,2048,1,64]{1,3,2,0:T(8,128)(2,1)} async-done(((bf16[16,2048,1,64]{1,3,2,0:T(8,128)(2,1)}), bf16[16,2048,1,64]{1,3,2,0:T(8,128)(2,1)}, u32[]{:S(2)}, u32[]{:S(2)}) %all-to-all-start.1) | async-done | bytes 4194336 | tf_op jit(solution)/shard_map/all_to_all | solution.py:12
  184.3 3.7 %copy.30 = bf16[128,8,8,256]{3,2,1,0:T(8,128)(2,1)S(1)} copy(bf16[128,8,8,256]{3,1,2,0:T(8,128)(2,1)} %bitcast.16) | data formatting | bytes 8388608
  188.0 2.8 copy.24
  190.8 5.0 %all-to-all-start.2 = ((bf16[8,256,1024]{1,2,0:T(8,128)(2,1)}), bf16[8,256,1024]{1,2,0:T(8,128)(2,1)}, u32[]{:S(2)}, u32[]{:S(2)}) async-start(bf16[8,256,1024]{1,2,0:T(8,128)(2,1)} %copy.24), calls=%async_computation.2 | async-start | bytes 8388608 | tf_op jit(solution)/shard_map/all_to_all | solution.py:28
  195.8 66.1 %all-to-all-done.2 = bf16[8,256,1024]{1,2,0:T(8,128)(2,1)} async-done(((bf16[8,256,1024]{1,2,0:T(8,128)(2,1)}), bf16[8,256,1024]{1,2,0:T(8,128)(2,1)}, u32[]{:S(2)}, u32[]{:S(2)}) %all-to-all-start.2) | async-done | bytes 4194336 | tf_op jit(solution)/shard_map/all_to_all | solution.py:28
  261.9 1.0 constant_dynamic-slice_fusion
  263.0 9.7 %convolution_multiply_fusion = f32[256,640]{1,0:T(8,128)} fusion(bf16[256,8192]{0,1:T(8,128)(2,1)} %bitcast.4, bf16[640,8192]{1,0:T(8,128)(2,1)} %param.12, bf16[256,640]{1,0:T(8,128)(2,1)S(1)} %fusion.2), kind=kOutput, calls=%fused_computation.1 | convolution fusion | flops 2684682240 | bytes 15663104 | tf_op jit(solution)/shard_map/dot_general | solution.py:51
  272.7 8.2 %reduce-scatter.2.cloned.1.call-done = bf16[256,512]{1,0:T(8,128)(2,1)} async-done(((bf16[256,8192]{1,0:T(8,128)(2,1)}), bf16[256,512]{1,0:T(8,128)(2,1)}) %reduce-scatter.2.cloned.1.call-update) | async-done | bytes 262160 | tf_op jit(solution)/shard_map/reduce_scatter | solution.py:40
  281.0 1.9 multiply_reduce_fusion
  282.9 31.1 %psum.7 = f32[256]{0:T(256)} all-reduce(f32[256]{0:T(256)S(1)} %get-tuple-element.3), channel_id=1, replica_groups=mesh['tok'=8,'feat'=16] {'feat'}, use_global_device_ids=true, to_apply=%region_3.0 | all-reduce | flops 256 | bytes 2048 | tf_op jit(solution)/shard_map/psum | solution.py:50
  (24 shorter events, 0.4 us)
Async XLA Ops:
  7.2 42.3 %all-gather.3.cloned.1.call-start = ((), (), s32[]{:S(2)}) async-start(), calls=%async_computation.5 | async-start | bytes 4456448 | tf_op jit(solution)/shard_map/all_gather | solution.py:20
  55.9 6.7 %copy-start.3 = (s32[2,20]{1,0:T(2,128)S(1)}, s32[2,20]{1,0:T(2,128)}, u32[]{:S(2)}) copy-start(s32[2,20]{1,0:T(2,128)} %param.9) | copy-start | bytes 484
  55.9 66.7 %copy-start.1 = (bf16[2048,64]{0,1:T(8,128)(2,1)S(1)}, bf16[2048,64]{0,1:T(8,128)(2,1)}, u32[]{:S(2)}) copy-start(bf16[2048,64]{0,1:T(8,128)(2,1)} %param.8) | copy-start | bytes 786436
  55.9 66.6 %all-to-all-start = ((bf16[8,256,1024]{2,1,0:T(8,128)(2,1)}), bf16[8,256,1024]{2,1,0:T(8,128)(2,1)}, u32[]{:S(2)}, u32[]{:S(2)}) async-start(bf16[8,256,1024]{2,1,0:T(8,128)(2,1)} %bitcast.27), calls=%async_computation | async-start | bytes 8388608 | tf_op jit(solution)/shard_map/all_to_all | solution.py:27
  125.0 59.3 %all-to-all-start.1 = ((bf16[16,2048,1,64]{1,3,2,0:T(8,128)(2,1)}), bf16[16,2048,1,64]{1,3,2,0:T(8,128)(2,1)}, u32[]{:S(2)}, u32[]{:S(2)}) async-start(bf16[16,2048,1,64]{1,3,2,0:T(8,128)(2,1)} %stack.3), calls=%async_computation.1 | async-start | bytes 8388608 | tf_op jit(solution)/shard_map/all_to_all | solution.py:12
  129.6 151.4 %reduce-scatter.2.cloned.1.call-start = ((), (), s32[]{:S(2)}) async-start(), calls=%async_computation.4 | async-start | bytes 4456448 | tf_op jit(solution)/shard_map/reduce_scatter | solution.py:40
  129.6 4.8 %copy-start.4 = (f32[640]{0:T(1024)S(1)}, f32[640]{0:T(1024)}, u32[]{:S(2)}) copy-start(f32[640]{0:T(1024)} %param.11) | copy-start | bytes 7684
  129.6 11.2 %slice-start = ((s8[10485760]{0:T(1024)(128)(4,1)}), s8[4194304]{0:T(1024)(128)(4,1)S(1)}, s32[]{:S(2)}) async-start(s8[10485760]{0:T(1024)(128)(4,1)} %bitcast.33), calls=%async_computation.6 | async-start | bytes 8388608
  132.4 2.0 copy-start
  134.4 6.5 %slice-start.1 = ((s8[10485760]{0:T(1024)(128)(4,1)}), s8[4194304]{0:T(1024)(128)(4,1)S(1)}, s32[]{:S(2)}) async-start(s8[10485760]{0:T(1024)(128)(4,1)} %bitcast.33), calls=%async_computation.7 | async-start | bytes 8388608
  134.4 6.5 %slice-start.2 = ((s8[10485760]{0:T(1024)(128)(4,1)}), s8[2097152]{0:T(1024)(128)(4,1)S(1)}, s32[]{:S(2)}) async-start(s8[10485760]{0:T(1024)(128)(4,1)} %bitcast.33), calls=%async_computation.8 | async-start | bytes 4194304
  190.8 71.1 %all-to-all-start.2 = ((bf16[8,256,1024]{1,2,0:T(8,128)(2,1)}), bf16[8,256,1024]{1,2,0:T(8,128)(2,1)}, u32[]{:S(2)}, u32[]{:S(2)}) async-start(bf16[8,256,1024]{1,2,0:T(8,128)(2,1)} %copy.24), calls=%async_computation.2 | async-start | bytes 8388608 | tf_op jit(solution)/shard_map/all_to_all | solution.py:28
  263.0 18.0 %copy-start.2 = (f32[512]{0:T(512)S(1)}, f32[512]{0:T(512)}, u32[]{:S(2)}) copy-start(f32[512]{0:T(512)} %param.13) | copy-start | bytes 6148
Sparse Core Ops, SparseCore 0:
  9.7 39.7 all-gather.2
  146.1 134.8 reduce-scatter.1
